TPU v7x, 256 devices: a whole 4x4x8 slice. The times are simulated.
256 devices in a mesh: ta: 64 (over y, z_lo, x, core), site: 4 (over z_hi).
Axes of the slice: x: 4, y: 4, z: 8 (z_hi: 4, z_lo: 2; z = z_hi * 2 + z_lo), core: 2. Of those that a mesh axis runs over, the one named last changes fastest.
Arguments:
- eigenvectors: bfloat16 [128, 192, 3, 4, 256], P('ta', None, None, 'site'), parts along dimension 0, may hold values from -6 to 6
- gauge_links: bfloat16 [128, 3, 3, 3, 4, 256], P('ta', None, None, None, 'site'), parts along dimension 0, may hold values from -2.5 to 2.5
- displacements: int32 [2, 3], replicated, may hold values from 0 to 3, as said below
- block_rows: int32 [4], replicated, may hold values from 0 to 191
Outputs:
- elementals: float32 [128, 4, 192, 384], P('ta', None, 'site'), parts along dimension 0
There are 64 independent parts, one for each index of `ta`. A program takes and returns all parts, laid end to end along the dimension named above; an argument that names none is the same for every part. Nothing has to cross between parts.
Inputs may be any that keep to these rules, and one draw needn't show every extreme that they name: `displacements`: each combination displaces at least one of its three vectors along the third dimension.
All inputs are finite; a program needn't handle non-finite values.
Results may differ from a plain program's by a relative error of at most 0.012.
Values may be sent and summed in bfloat16 or wider, within the bound.
A program may use at most 64 MiB of HBM per device.

v0:
```python
import functools
import math

import jax
import jax.numpy as jnp
from jax import lax
from jax.experimental import pallas as pl
from jax.experimental.pallas import tpu as pltpu
from jax.sharding import PartitionSpec as P

LX = 16
RING = 4
LINK_ROWS = 24
NT = (((1,), (1,)), ((), ()))


def shift_matrix(moved_x, moved_y, sites):
    here = lax.broadcasted_iota(jnp.int32, (1, sites), 1)
    x, y = here % LX, here // LX
    rows = sites // LX
    there = ((y + moved_y + rows) % rows) * LX + (x + moved_x + LX) % LX
    source = lax.broadcasted_iota(jnp.int32, (sites, sites), 0)
    return jnp.where(source == there, 1.0, 0.0).astype(jnp.bfloat16)


def as_int(condition):
    return jnp.where(condition, 1, 0)


def kernel(scale, disp, rows, psi, links, out, g, jb, sb, s32, u32, l32, w32, j32, x, perm,
           local_sem, send, recv, small_send, small_recv):
    me = lax.axis_index("site")
    after, behind, across = (me + 1) % RING, (me + 3) % RING, (me + 2) % RING
    block = jb.shape[3]
    sites = jb.shape[4]

    def own(offset):
        return (me + offset) % RING

    fills = []
    for chunk in range(RING):
        fills.append(pltpu.make_async_copy(
            psi.at[:, :, pl.ds(chunk * block, block), :], g.at[0, chunk], local_sem.at[chunk]))
    fills.append(pltpu.make_async_copy(
        psi.at[:, :, pl.ds(pl.multiple_of(me * block, block), block), :], jb.at[0], local_sem.at[RING]))
    for fill in fills:
        fill.start()

    barrier = pltpu.get_barrier_semaphore()
    for peer in (after, behind, across):
        pl.semaphore_signal(barrier, inc=1, device_id={"site": peer})
    pl.semaphore_wait(barrier, 3)
    for fill in fills:
        fill.wait()

    def carry(lane, number, source, target, peer):
        return pltpu.make_async_remote_copy(
            src_ref=source, dst_ref=target,
            send_sem=send.at[lane, number], recv_sem=recv.at[lane, number],
            device_id={"site": peer})

    up = [
        carry(0, 0, g.at[0, own(2)], g.at[3, own(2)], after),
        carry(0, 1, g.at[0, own(1)], jb.at[3], after),
        carry(0, 2, g.at[3, own(1)], jb.at[2], after),
        carry(0, 3, g.at[0, own(0)], g.at[3, own(0)], after),
        carry(0, 4, g.at[0, own(3)], g.at[3, own(3)], after),
        carry(0, 5, jb.at[3], g.at[2, own(0)], after),
    ]
    down = [
        carry(1, 0, g.at[0, own(3)], jb.at[1], behind),
        carry(1, 1, g.at[0, own(0)], g.at[1, own(0)], behind),
        carry(1, 2, g.at[0, own(1)], g.at[1, own(1)], behind),
        carry(1, 3, g.at[0, own(2)], g.at[1, own(2)], behind),
        carry(1, 4, jb.at[1], g.at[2, own(0)], behind),
        carry(1, 5, g.at[1, own(1)], g.at[2, own(1)], behind),
    ]
    up[0].start()
    down[0].start()
    up[1].start()
    down[1].start()

    s32[...] = jnp.zeros_like(s32)
    for direction in range(3):
        for a in range(3):
            for b in range(3):
                at = direction * LINK_ROWS + (a * 3 + b) * 2
                s32[at:at + 2] = links[direction, a, b].astype(jnp.float32)
    vectors = RING * block
    number = lax.broadcasted_iota(jnp.int32, (LINK_ROWS, vectors), 0)
    column = lax.broadcasted_iota(jnp.int32, (LINK_ROWS, vectors), 1)
    wanted = jnp.zeros((LINK_ROWS, vectors), jnp.int32)
    for i in range(4):
        wanted = jnp.where(number % 4 == i, rows[i], wanted)
    found = column == wanted
    picked = jnp.zeros((LINK_ROWS, sites), jnp.float32)
    for q in range(2):
        for c in range(3):
            pick = jnp.where(found & (number // 4 == q * 3 + c), 1.0, 0.0).astype(jnp.bfloat16)
            whole = jnp.concatenate([g[0, chunk, q, c] for chunk in range(RING)], axis=0)
            picked += jnp.dot(pick, whole, preferred_element_type=jnp.float32)
    s32[3 * LINK_ROWS:4 * LINK_ROWS] = picked
    sb[0] = s32[...].astype(jnp.bfloat16)
    small = []
    for k, (slot, peer) in enumerate(((3, after), (1, behind), (2, across))):
        small.append(pltpu.make_async_remote_copy(
            src_ref=sb.at[0], dst_ref=sb.at[slot],
            send_sem=small_send.at[k], recv_sem=small_recv.at[k],
            device_id={"site": peer}))
        small[-1].start()

    for m in range(2):
        d1, d2, d3 = disp[m, 0], disp[m, 1], disp[m, 2]
        back_x, back_y = as_int(d3 == 1), as_int(d3 == 2)
        perm[m, 0] = shift_matrix(-back_x, -back_y, sites)
        perm[m, 1] = shift_matrix(as_int(d2 == 1) - back_x, as_int(d2 == 2) - back_y, sites)
        perm[m, 2] = shift_matrix(as_int(d1 == 1) - back_x, as_int(d1 == 2) - back_y, sites)

    up[0].wait_recv()
    up[2].start()
    up[3].start()
    down[0].wait_recv()
    down[2].start()
    up[1].wait_recv()
    up[4].start()
    up[5].start()
    down[1].wait_recv()
    down[3].start()
    down[4].start()
    down[5].start()
    for message in small:
        message.wait_recv()
    up[2].wait_recv()
    for slot in range(1, RING):
        g[slot, me] = jb[slot]

    def build(step, carried):
        slot, m = step // 2, step % 2
        d1, d2, d3 = disp[m, 0], disp[m, 1], disp[m, 2]
        base = (slot + RING - as_int(d3 == 3)) % RING
        mid = (base + as_int(d2 == 3)) % RING
        left = (base + as_int(d1 == 3)) % RING
        moved = jnp.dot(sb[base], perm[m, 0], preferred_element_type=jnp.float32)
        entry = lax.broadcasted_iota(jnp.int32, (LINK_ROWS, sites), 0)
        identity = jnp.where((entry == 0) | (entry == 8) | (entry == 16), 1.0, 0.0)
        for k, d in enumerate((d1, d2, d3)):
            chosen = identity
            for direction in range(3):
                candidate = moved[direction * LINK_ROWS:(direction + 1) * LINK_ROWS]
                chosen = jnp.where(d == direction + 1, candidate, chosen)
            u32[k] = chosen
        l32[...] = scale * jnp.dot(
            sb[left, 3 * LINK_ROWS:4 * LINK_ROWS, :], perm[m, 2], preferred_element_type=jnp.float32)
        j32[...] = jnp.dot(
            jb[mid].reshape(6 * block, sites), perm[m, 1],
            preferred_element_type=jnp.float32).reshape(j32.shape)

        def link(k, a, b):
            at = (a * 3 + b) * 2
            return (u32[k, at:at + 1, :], u32[k, at + 1:at + 2, :])

        def times(one, two):
            return (one[0] * two[0] - one[1] * two[1], one[0] * two[1] + one[1] * two[0])

        def plus(one, two):
            return (one[0] + two[0], one[1] + two[1])

        def minus(one, two):
            return (one[0] - two[0], one[1] - two[1])

        source = [(l32[4 * b:4 * b + 4, :], l32[12 + 4 * b:16 + 4 * b, :]) for b in range(3)]
        lefts = []
        for a in range(3):
            total = times(source[0], link(0, a, 0))
            for b in (1, 2):
                total = plus(total, times(source[b], link(0, a, b)))
            lefts.append(total)
        for d in range(3):
            triple = []
            for b in range(3):
                one, two = (b + 1) % 3, (b + 2) % 3
                triple.append(minus(times(lefts[two], link(2, one, d)), times(lefts[one], link(2, two, d))))
            for e in range(3):
                total = times(triple[0], link(1, 0, e))
                for b in (1, 2):
                    total = plus(total, times(triple[b], link(1, b, e)))
                w32[d, e, 0, 0:4, :] = total[0]
                w32[d, e, 1, 0:4, :] = total[1]

        for half in range(sites // 128):
            lanes = slice(half * 128, half * 128 + 128)
            re = [j32[e, :, lanes] for e in range(3)]
            im = [j32[3 + e, :, lanes] for e in range(3)]
            for d in range(3):
                for i in range(4):
                    total = None
                    for e in range(3):
                        w = (w32[d, e, 0, i:i + 1, lanes], w32[d, e, 1, i:i + 1, lanes])
                        term = times((re[e], im[e]), w)
                        total = term if total is None else plus(total, term)
                    place = slice(d * sites + half * 128, d * sites + half * 128 + 128)
                    for q in range(2):
                        x[slot, q, m, i * block:(i + 1) * block, place] = total[q].astype(jnp.bfloat16)
        return carried

    lax.fori_loop(0, 2 * RING, build, 0)

    def contract(slot):
        first, second = [], []
        for c in range(3):
            re = [g[slot, chunk, 0, c] for chunk in range(RING)]
            im = [g[slot, chunk, 1, c] for chunk in range(RING)]
            first.append(jnp.concatenate(re + im, axis=0))
            second.append(jnp.concatenate([-part for part in im] + re, axis=0))
        total = None
        for q, parts in enumerate((first, second)):
            left = x[slot, q].reshape(8 * block, 3 * sites)
            product = lax.dot_general(
                left, jnp.concatenate(parts, axis=1), NT, preferred_element_type=jnp.float32)
            total = product if total is None else total + product
        return total.reshape(out.shape)

    out[...] = contract(0)
    for k in (2, 3):
        down[k].wait_recv()
    out[...] += contract(1)
    for k in (3, 4):
        up[k].wait_recv()
    out[...] += contract(3)
    up[5].wait_recv()
    down[4].wait_recv()
    down[5].wait_recv()
    out[...] += contract(2)
    for copy in up + down + small:
        copy.wait_send()


def on_device(eigenvectors, gauge_links, displacements, block_rows):
    psi = jnp.transpose(eigenvectors[:, :, :, 0, :], (0, 2, 1, 3))
    links = jnp.transpose(gauge_links[:, :, :, :, 0, :], (1, 2, 3, 0, 4))
    _, colors, vectors, sites = psi.shape
    block = vectors // RING
    scale = 1.0 / math.sqrt(24.0 * sites * RING)
    f32, bf16 = jnp.float32, jnp.bfloat16
    vmem = pl.BlockSpec(memory_space=pltpu.VMEM)
    smem = pl.BlockSpec(memory_space=pltpu.SMEM)
    return pl.pallas_call(
        functools.partial(kernel, scale),
        out_shape=jax.ShapeDtypeStruct((2, 4, block, 2 * vectors), f32),
        in_specs=[smem, smem, pl.BlockSpec(memory_space=pl.ANY), vmem],
        out_specs=vmem,
        scratch_shapes=[
            pltpu.VMEM((RING, RING, 2, 3, block, sites), bf16),
            pltpu.VMEM((RING, 2, 3, block, sites), bf16),
            pltpu.VMEM((RING, 4 * LINK_ROWS, sites), bf16),
            pltpu.VMEM((4 * LINK_ROWS, sites), f32),
            pltpu.VMEM((3, LINK_ROWS, sites), f32),
            pltpu.VMEM((LINK_ROWS, sites), f32),
            pltpu.VMEM((3, 3, 2, 8, sites), f32),
            pltpu.VMEM((6, block, sites), f32),
            pltpu.VMEM((RING, 2, 2, 4 * block, 3 * sites), bf16),
            pltpu.VMEM((2, 3, sites, sites), bf16),
            pltpu.SemaphoreType.DMA((RING + 1,)),
            pltpu.SemaphoreType.DMA((2, 6)),
            pltpu.SemaphoreType.DMA((2, 6)),
            pltpu.SemaphoreType.DMA((3,)),
            pltpu.SemaphoreType.DMA((3,)),
        ],
        compiler_params=pltpu.CompilerParams(
            collective_id=0, has_side_effects=True, vmem_limit_bytes=40 * 1024 * 1024),
    )(displacements, block_rows, psi, links)


def solution(mesh):
    return jax.shard_map(
        on_device,
        mesh=mesh,
        in_specs=(
            P("ta", None, None, "site", None),
            P("ta", None, None, None, "site", None),
            P(),
            P(),
        ),
        out_specs=P("ta", None, "site", None),
        check_vma=False,
    )
```

profile of v0, /device:TPU:35, one launch (start us, length us, event | category | flops | bytes accessed | tf_op | source)
XLA Modules:
  0.0 55.3 jit_solution(5288249326776193764)
XLA Ops:
  0.0 0.0 copy-start.2
  0.0 0.0 copy-start.3
  0.0 0.7 %copy-done.2 = s32[2,3]{1,0:T(2,128)S(1)} copy-done((s32[2,3]{1,0:T(2,128)S(1)}, s32[2,3]{1,0:T(2,128)}, u32[]{:S(2)}) %copy-start.2) | copy-done | bytes 48
  0.7 0.0 copy-done.3
  0.7 0.0 copy-start
  0.7 1.1 %copy-done = bf16[2,192,3,1,256]{4,1,3,2,0:T(8,128)(2,1)S(1)} copy-done((bf16[2,192,3,1,256]{4,1,3,2,0:T(8,128)(2,1)S(1)}, bf16[2,192,3,1,256]{4,1,3,2,0:T(8,128)(2,1)}, u32[]{:S(2)}) %copy-start) | copy-done | bytes 589848
  1.7 0.0 copy-start.1
  1.8 0.7 %copy-done.1 = bf16[2,3,3,3,1,256]{5,0,4,3,2,1:T(2,128)(2,1)S(1)} copy-done((bf16[2,3,3,3,1,256]{5,0,4,3,2,1:T(2,128)(2,1)S(1)}, bf16[2,3,3,3,1,256]{5,0,4,3,2,1:T(2,128)(2,1)}, u32[]{:S(2)}) %copy-start.1) | copy-done | bytes 27672
  2.5 52.0 %shard_map.46 = f32[2,4,48,384]{3,2,1,0:T(8,128)S(1)} custom-call(s32[2,3]{1,0:T(2,128)S(1)} %copy-done.2, s32[4]{0:T(128)S(1)} %copy-done.3, bf16[2,3,192,256]{3,2,1,0:T(8,128)(2,1)S(1)} %bitcast.6, bf16[3,3,3,2,256]{4,3,2,1,0:T(2,128)(2,1)S(1)} %bitcast.7), custom_call_target="tpu_custom_call" | custom-call | tf_op jit(solution)/shard_map/pallas_call | solution.py:247
  54.5 0.8 %copy.6 = f32[2,4,48,384]{3,2,1,0:T(8,128)} copy(f32[2,4,48,384]{3,2,1,0:T(8,128)S(1)} %shard_map.46) | data formatting | bytes 1179648
Async XLA Ops:
  0.0 0.7 %copy-start.2 = (s32[2,3]{1,0:T(2,128)S(1)}, s32[2,3]{1,0:T(2,128)}, u32[]{:S(2)}) copy-start(s32[2,3]{1,0:T(2,128)} %disp.1) | copy-start | bytes 76
  0.0 0.7 %copy-start.3 = (s32[4]{0:T(128)S(1)}, s32[4]{0:T(128)}, u32[]{:S(2)}) copy-start(s32[4]{0:T(128)} %rows.1) | copy-start | bytes 52
  0.7 1.1 %copy-start = (bf16[2,192,3,1,256]{4,1,3,2,0:T(8,128)(2,1)S(1)}, bf16[2,192,3,1,256]{4,1,3,2,0:T(8,128)(2,1)}, u32[]{:S(2)}) copy-start(bf16[2,192,3,1,256]{4,1,3,2,0:T(8,128)(2,1)} %param.4) | copy-start | bytes 1769476
  1.7 0.7 %copy-start.1 = (bf16[2,3,3,3,1,256]{5,0,4,3,2,1:T(2,128)(2,1)S(1)}, bf16[2,3,3,3,1,256]{5,0,4,3,2,1:T(2,128)(2,1)}, u32[]{:S(2)}) copy-start(bf16[2,3,3,3,1,256]{5,0,4,3,2,1:T(2,128)(2,1)} %param.5) | copy-start | bytes 82948
where the time goes:
time: 55.5 us; the launch traced here: 55.3 us
  Pallas kernels  52 us (94%)
  local copies, waits for them, and re-layouts  3.31 us (6%)
    pallas_call x1, Pallas kernels, on_device(): pl.pallas_call(functools.partial(kernel, scale), out_shape=jax.ShapeDtype...  52 us
    unnamed x9, local copies, waits for them, and re-layouts  3.31 us

commit v1 on v0

v1 whole, which is shorter than its diff:
```python
import functools
import math

import jax
import jax.numpy as jnp
from jax import lax
from jax.experimental import pallas as pl
from jax.experimental.pallas import tpu as pltpu
from jax.sharding import PartitionSpec as P

LX = 16
RING = 4
LINK_ROWS = 18
SMALL_ROWS = 80
NT = (((1,), (1,)), ((), ()))


def shift_matrix(moved_x, moved_y, sites):
    here = lax.broadcasted_iota(jnp.int32, (1, sites), 1)
    x, y = here % LX, here // LX
    rows = sites // LX
    there = ((y + moved_y + rows) % rows) * LX + (x + moved_x + LX) % LX
    source = lax.broadcasted_iota(jnp.int32, (sites, sites), 0)
    return jnp.where(source == there, 1.0, 0.0).astype(jnp.bfloat16)


def as_int(condition):
    return jnp.where(condition, 1, 0)


def times(one, two):
    return (one[0] * two[0] - one[1] * two[1], one[0] * two[1] + one[1] * two[0])


def plus(one, two):
    return (one[0] + two[0], one[1] + two[1])


def minus(one, two):
    return (one[0] - two[0], one[1] - two[1])


def kernel(scale, disp_hbm, rows_hbm, psi, links_hbm, out, disp, rows, links, g, sb, s32, u32, l32, w32, j32, x,
           perm, put, got, local_sem, halo_send, halo_recv, sum_send, sum_recv):
    me = lax.axis_index("site")
    core = lax.axis_index("ta") % 2
    after, behind = (me + 1) % RING, (me + RING - 1) % RING
    block = g.shape[4]
    sites = g.shape[5]

    fills = [
        pltpu.make_async_copy(psi.at[:, :, pl.ds(chunk * block, block), :], g.at[0, chunk], local_sem.at[chunk])
        for chunk in range(RING)
    ]
    fills.append(pltpu.make_async_copy(links_hbm, links, local_sem.at[RING]))
    fills.append(pltpu.make_async_copy(rows_hbm, rows, local_sem.at[RING + 1]))
    fills.append(pltpu.make_async_copy(disp_hbm, disp, local_sem.at[RING + 2]))
    for fill in fills:
        fill.start()
    barrier = pltpu.get_barrier_semaphore()
    for peer in (after, behind):
        pl.semaphore_signal(barrier, inc=1, device_id={"site": peer})
    pl.semaphore_wait(barrier, 2)
    for fill in fills:
        fill.wait()

    reader = (me + RING - 1 + 2 * core) % RING
    order = (2, 3, 1, 0)
    halo = []
    for number, offset in enumerate(order):
        sent = (reader + offset) % RING
        halo.append(pltpu.make_async_remote_copy(
            src_ref=g.at[0, sent], dst_ref=g.at[1, sent],
            send_sem=halo_send.at[number], recv_sem=halo_recv.at[number], device_id={"site": reader}))
    halo[0].start()

    s32[3 * LINK_ROWS:56] = jnp.zeros((56 - 3 * LINK_ROWS, sites), jnp.float32)
    for direction in range(3):
        for a in range(3):
            for b in range(3):
                at = direction * LINK_ROWS + (a * 3 + b) * 2
                s32[at:at + 2] = links[direction, a, b].astype(jnp.float32)
    vectors = RING * block
    number = lax.broadcasted_iota(jnp.int32, (24, vectors), 0)
    column = lax.broadcasted_iota(jnp.int32, (24, vectors), 1)
    wanted = jnp.zeros((24, vectors), jnp.int32)
    for i in range(4):
        wanted = jnp.where(number % 4 == i, rows[i], wanted)
    found = column == wanted
    picked = jnp.zeros((24, sites), jnp.float32)
    for q in range(2):
        for c in range(3):
            pick = jnp.where(found & (number // 4 == q * 3 + c), 1.0, 0.0).astype(jnp.bfloat16)
            whole = jnp.concatenate([g[0, chunk, q, c] for chunk in range(RING)], axis=0)
            picked += jnp.dot(pick, whole, preferred_element_type=jnp.float32)
    s32[56:80] = picked
    sb[0] = s32[...].astype(jnp.bfloat16)
    small = pltpu.make_async_remote_copy(
        src_ref=sb.at[0], dst_ref=sb.at[1],
        send_sem=halo_send.at[RING], recv_sem=halo_recv.at[RING], device_id={"site": reader})
    small.start()
    for copy in halo[1:]:
        copy.start()

    for m in range(2):
        d1, d2, d3 = disp[m, 0], disp[m, 1], disp[m, 2]
        back_x, back_y = as_int(d3 == 1), as_int(d3 == 2)
        perm[m, 0] = shift_matrix(-back_x, -back_y, sites)
        perm[m, 1] = shift_matrix(as_int(d2 == 1) - back_x, as_int(d2 == 2) - back_y, sites)
        perm[m, 2] = shift_matrix(as_int(d1 == 1) - back_x, as_int(d1 == 2) - back_y, sites)

    small.wait_recv()

    def imported(d):
        return (core + as_int(d == 3)) % 2 == 1

    def weights(m, carried):
        d1, d2, d3 = disp[m, 0], disp[m, 1], disp[m, 2]
        own, other = sb[0].astype(jnp.float32), sb[1].astype(jnp.float32)
        near = jnp.where(core == 1, other, own).astype(jnp.bfloat16)
        left = jnp.where(imported(d1), other, own)[56:80].astype(jnp.bfloat16)
        moved = jnp.dot(near, perm[m, 0], preferred_element_type=jnp.float32)
        entry = lax.broadcasted_iota(jnp.int32, (LINK_ROWS, sites), 0)
        identity = jnp.where((entry == 0) | (entry == 8) | (entry == 16), 1.0, 0.0)
        for k, d in enumerate((d1, d2, d3)):
            chosen = identity
            for direction in range(3):
                candidate = moved[direction * LINK_ROWS:(direction + 1) * LINK_ROWS]
                chosen = jnp.where(d == direction + 1, candidate, chosen)
            u32[k, 0:LINK_ROWS] = chosen
        l32[...] = scale * jnp.dot(left, perm[m, 2], preferred_element_type=jnp.float32)

        def link(k, a, b):
            at = (a * 3 + b) * 2
            return (u32[k, at:at + 1, :], u32[k, at + 1:at + 2, :])

        source = [(l32[4 * b:4 * b + 4, :], l32[12 + 4 * b:16 + 4 * b, :]) for b in range(3)]
        lefts = []
        for a in range(3):
            total = times(source[0], link(0, a, 0))
            for b in (1, 2):
                total = plus(total, times(source[b], link(0, a, b)))
            lefts.append(total)
        for d in range(3):
            triple = []
            for b in range(3):
                one, two = (b + 1) % 3, (b + 2) % 3
                triple.append(minus(times(lefts[two], link(2, one, d)), times(lefts[one], link(2, two, d))))
            for e in range(3):
                total = times(triple[0], link(1, 0, e))
                for b in (1, 2):
                    total = plus(total, times(triple[b], link(1, b, e)))
                w32[m, d, e, 0, 0:4, :] = total[0]
                w32[m, d, e, 1, 0:4, :] = total[1]
        return carried

    lax.fori_loop(0, 2, weights, 0)

    def build(slot, chunk):
        def one(m, carried):
            mine = g[0, chunk].reshape(6 * block, sites)
            theirs = g[1, chunk].reshape(6 * block, sites)
            mid = jnp.where(imported(disp[m, 1]), theirs, mine)
            j32[...] = jnp.dot(mid, perm[m, 1], preferred_element_type=jnp.float32).reshape(j32.shape)
            for half in range(sites // 128):
                lanes = slice(half * 128, half * 128 + 128)
                re = [j32[e, :, lanes] for e in range(3)]
                im = [j32[3 + e, :, lanes] for e in range(3)]
                for d in range(3):
                    for i in range(4):
                        total = None
                        for e in range(3):
                            w = (w32[m, d, e, 0, i:i + 1, lanes], w32[m, d, e, 1, i:i + 1, lanes])
                            term = times((re[e], im[e]), w)
                            total = term if total is None else plus(total, term)
                        place = slice(d * sites + half * 128, d * sites + half * 128 + 128)
                        for q in range(2):
                            x[m, slot, q, i * block:(i + 1) * block, place] = total[q].astype(jnp.bfloat16)
            return carried

        lax.fori_loop(0, 2, one, 0)

    for copy, offset in zip(halo, order):
        copy.wait_recv()
        build(offset, (me + offset) % RING)

    def contract(m, slots):
        far = (core + as_int(disp[m, 2] == 3)) % 2
        first, second = [], []
        for c in range(3):
            re = [g[far, chunk, 0, c] for chunk in range(RING)]
            im = [g[far, chunk, 1, c] for chunk in range(RING)]
            first.append(jnp.concatenate(re + im, axis=0))
            second.append(jnp.concatenate([-part for part in im] + re, axis=0))
        total = None
        for q, parts in enumerate((first, second)):
            left = jnp.concatenate([x[m, slot, q] for slot in slots], axis=0)
            product = lax.dot_general(
                left, jnp.concatenate(parts, axis=1), NT, preferred_element_type=jnp.float32)
            total = product if total is None else total + product
        rows_each = 4 * block
        return [total[k * rows_each:(k + 1) * rows_each].reshape(4, block, 2 * vectors) for k in range(2)]

    def carry(lane, step, source, peer):
        return pltpu.make_async_remote_copy(
            src_ref=put.at[lane, step], dst_ref=got.at[lane, step],
            send_sem=sum_send.at[lane, step], recv_sem=sum_recv.at[lane, step], device_id={"site": peer})

    up = [carry(0, step, None, after) for step in range(3)]
    down = [carry(1, step, None, behind) for step in range(3)]

    across, below = contract(0, (2, 3))
    put[0, 0] = across.astype(jnp.bfloat16)
    up[0].start()
    put[1, 1] = below.astype(jnp.bfloat16)
    across, above = contract(1, (2, 1))
    put[1, 0] = across.astype(jnp.bfloat16)
    down[0].start()
    put[0, 1] = above.astype(jnp.bfloat16)
    up[1].start()
    down[1].start()
    above, own = contract(0, (1, 0))
    out[0] = own
    up[0].wait_recv()
    put[0, 2] = (above + got[0, 0].astype(jnp.float32)).astype(jnp.bfloat16)
    up[2].start()
    below, own = contract(1, (3, 0))
    out[1] = own
    down[0].wait_recv()
    put[1, 2] = (below + got[1, 0].astype(jnp.float32)).astype(jnp.bfloat16)
    down[2].start()
    up[1].wait_recv()
    out[1] += got[0, 1].astype(jnp.float32)
    down[1].wait_recv()
    out[0] += got[1, 1].astype(jnp.float32)
    up[2].wait_recv()
    out[0] += got[0, 2].astype(jnp.float32)
    down[2].wait_recv()
    out[1] += got[1, 2].astype(jnp.float32)
    for copy in halo + [small] + up + down:
        copy.wait_send()


def on_device(eigenvectors, gauge_links, displacements, block_rows):
    psi = jnp.transpose(eigenvectors[:, :, :, 0, :], (0, 2, 1, 3))
    links = jnp.transpose(gauge_links[:, :, :, :, 0, :], (1, 2, 3, 0, 4))
    _, colors, vectors, sites = psi.shape
    block = vectors // RING
    scale = 1.0 / math.sqrt(24.0 * sites * RING)
    f32, bf16 = jnp.float32, jnp.bfloat16
    hbm = pl.BlockSpec(memory_space=pltpu.HBM)
    return pl.pallas_call(
        functools.partial(kernel, scale),
        out_shape=jax.ShapeDtypeStruct((2, 4, block, 2 * vectors), f32),
        in_specs=[hbm, hbm, hbm, hbm],
        out_specs=pl.BlockSpec(memory_space=pltpu.VMEM),
        scratch_shapes=[
            pltpu.SMEM(displacements.shape, displacements.dtype),
            pltpu.SMEM(block_rows.shape, block_rows.dtype),
            pltpu.VMEM(links.shape, bf16),
            pltpu.VMEM((2, RING, 2, 3, block, sites), bf16),
            pltpu.VMEM((2, SMALL_ROWS, sites), bf16),
            pltpu.VMEM((SMALL_ROWS, sites), f32),
            pltpu.VMEM((3, 24, sites), f32),
            pltpu.VMEM((24, sites), f32),
            pltpu.VMEM((2, 3, 3, 2, 8, sites), f32),
            pltpu.VMEM((6, block, sites), f32),
            pltpu.VMEM((2, RING, 2, 4 * block, 3 * sites), bf16),
            pltpu.VMEM((2, 3, sites, sites), bf16),
            pltpu.VMEM((2, 3, 4, block, 2 * vectors), bf16),
            pltpu.VMEM((2, 3, 4, block, 2 * vectors), bf16),
            pltpu.SemaphoreType.DMA((RING + 3,)),
            pltpu.SemaphoreType.DMA((RING + 1,)),
            pltpu.SemaphoreType.DMA((RING + 1,)),
            pltpu.SemaphoreType.DMA((2, 3)),
            pltpu.SemaphoreType.DMA((2, 3)),
        ],
        compiler_params=pltpu.CompilerParams(
            collective_id=0, has_side_effects=True, vmem_limit_bytes=63 * 1024 * 1024 + 512 * 1024),
    )(displacements, block_rows, psi, links)


def solution(mesh):
    return jax.shard_map(
        on_device,
        mesh=mesh,
        in_specs=(
            P("ta", None, None, "site", None),
            P("ta", None, None, None, "site", None),
            P(),
            P(),
        ),
        out_specs=P("ta", None, "site", None),
        check_vma=False,
    )
```

time: 55.5 us -> 47.7 us (0.86)
  the two profiles are of different devices: /device:TPU:35 before, /device:TPU:10 now
where the time goes in v1:
time: 47.7 us; the launch traced here: 47.6 us
  Pallas kernels  45.6 us (96%)
  local copies, waits for them, and re-layouts  1.92 us (4%)
    pallas_call x1, Pallas kernels, on_device(): pl.pallas_call(functools.partial(kernel, scale), out_shape=jax.ShapeDtype...  45.6 us
    unnamed x1, local copies, waits for them, and re-layouts  1.92 us

profile of v1, /device:TPU:10, one launch (start us, length us, event | category | flops | bytes accessed | tf_op | source)
XLA Modules:
  0.0 47.6 jit_solution(18359528759047679147)
XLA Ops:
  0.0 45.6 %shard_map.46 = f32[2,4,48,384]{3,2,1,0:T(8,128)} custom-call(s32[2,3]{1,0:T(2,128)} %disp_hbm.1, s32[4]{0:T(128)} %rows_hbm.1, bf16[2,3,192,256]{3,2,1,0:T(8,128)(2,1)} %bitcast.6, bf16[3,3,3,2,256]{4,3,2,1,0:T(2,128)(2,1)} %bitcast.7), custom_call_target="tpu_custom_call" | custom-call | tf_op jit(solution)/shard_map/pallas_call | solution.py:252
  45.6 1.9 %copy.6 = f32[2,4,48,384]{3,2,1,0:T(8,128)} copy(f32[2,4,48,384]{3,2,1,0:T(8,128)} %shard_map.46) | data formatting | bytes 1179648

commit v2 on v1

--- a/solution.py
+++ b/solution.py
@@ -11,7 +11,8 @@
 LX = 16
 RING = 4
 LINK_ROWS = 18
-SMALL_ROWS = 80
+TABLE_ROWS = 56
+PARTS = 1
 NT = (((1,), (1,)), ((), ()))
 
 
@@ -40,8 +41,8 @@
     return (one[0] - two[0], one[1] - two[1])
 
 
-def kernel(scale, disp_hbm, rows_hbm, psi, links_hbm, out, disp, rows, links, g, sb, s32, u32, l32, w32, j32, x,
-           perm, put, got, local_sem, halo_send, halo_recv, sum_send, sum_recv):
+def kernel(scale, disp_hbm, rows_hbm, psi, links_hbm, out, disp, rows, links, g, lb, kb, s32, u32, l32, w32, j32, x,
+           perm, put, got, held, local_sem, halo_send, halo_recv, sum_send, sum_recv, ready):
     me = lax.axis_index("site")
     core = lax.axis_index("ta") % 2
     after, behind = (me + 1) % RING, (me + RING - 1) % RING
@@ -57,24 +58,25 @@
     fills.append(pltpu.make_async_copy(disp_hbm, disp, local_sem.at[RING + 2]))
     for fill in fills:
         fill.start()
+    reader = (me + RING - 1 + 2 * core) % RING
+    writer = (me + 1 + 2 * core) % RING
     barrier = pltpu.get_barrier_semaphore()
-    for peer in (after, behind):
-        pl.semaphore_signal(barrier, inc=1, device_id={"site": peer})
-    pl.semaphore_wait(barrier, 2)
-    for fill in fills:
-        fill.wait()
-
-    reader = (me + RING - 1 + 2 * core) % RING
+    pl.semaphore_signal(barrier, inc=1, device_id={"site": writer})
+    pl.semaphore_wait(barrier, 1)
+    pl.semaphore_signal(ready, inc=1, device_id={"site": reader})
+
     order = (2, 3, 1, 0)
     halo = []
     for number, offset in enumerate(order):
         sent = (reader + offset) % RING
         halo.append(pltpu.make_async_remote_copy(
-            src_ref=g.at[0, sent], dst_ref=g.at[1, sent],
+            src_ref=psi.at[:, :, pl.ds(pl.multiple_of(sent * block, block), block), :], dst_ref=g.at[1, sent],
             send_sem=halo_send.at[number], recv_sem=halo_recv.at[number], device_id={"site": reader}))
     halo[0].start()
-
-    s32[3 * LINK_ROWS:56] = jnp.zeros((56 - 3 * LINK_ROWS, sites), jnp.float32)
+    for fill in fills:
+        fill.wait()
+
+    s32[3 * LINK_ROWS:] = jnp.zeros((TABLE_ROWS - 3 * LINK_ROWS, sites), jnp.float32)
     for direction in range(3):
         for a in range(3):
             for b in range(3):
@@ -93,12 +95,18 @@
             pick = jnp.where(found & (number // 4 == q * 3 + c), 1.0, 0.0).astype(jnp.bfloat16)
             whole = jnp.concatenate([g[0, chunk, q, c] for chunk in range(RING)], axis=0)
             picked += jnp.dot(pick, whole, preferred_element_type=jnp.float32)
-    s32[56:80] = picked
-    sb[0] = s32[...].astype(jnp.bfloat16)
-    small = pltpu.make_async_remote_copy(
-        src_ref=sb.at[0], dst_ref=sb.at[1],
-        send_sem=halo_send.at[RING], recv_sem=halo_recv.at[RING], device_id={"site": reader})
-    small.start()
+    lb[0] = picked.astype(jnp.bfloat16)
+    kb[0] = s32[...].astype(jnp.bfloat16)
+    small = [pltpu.make_async_remote_copy(
+        src_ref=buffer.at[0], dst_ref=buffer.at[1],
+        send_sem=halo_send.at[RING + number], recv_sem=halo_recv.at[RING + number], device_id={"site": reader})
+        for number, buffer in enumerate((lb, kb))]
+    small[0].start()
+
+    @pl.when(core == 1)
+    def _():
+        small[1].start()
+
     for copy in halo[1:]:
         copy.start()
 
@@ -109,17 +117,19 @@
         perm[m, 1] = shift_matrix(as_int(d2 == 1) - back_x, as_int(d2 == 2) - back_y, sites)
         perm[m, 2] = shift_matrix(as_int(d1 == 1) - back_x, as_int(d1 == 2) - back_y, sites)
 
-    small.wait_recv()
+    small[0].wait_recv()
+
+    @pl.when(core == 1)
+    def _():
+        small[1].wait_recv()
 
     def imported(d):
         return (core + as_int(d == 3)) % 2 == 1
 
     def weights(m, carried):
         d1, d2, d3 = disp[m, 0], disp[m, 1], disp[m, 2]
-        own, other = sb[0].astype(jnp.float32), sb[1].astype(jnp.float32)
-        near = jnp.where(core == 1, other, own).astype(jnp.bfloat16)
-        left = jnp.where(imported(d1), other, own)[56:80].astype(jnp.bfloat16)
-        moved = jnp.dot(near, perm[m, 0], preferred_element_type=jnp.float32)
+        moved = jnp.dot(kb[core], perm[m, 0], preferred_element_type=jnp.float32)
+        left = lb[(core + as_int(d1 == 3)) % 2]
         entry = lax.broadcasted_iota(jnp.int32, (LINK_ROWS, sites), 0)
         identity = jnp.where((entry == 0) | (entry == 8) | (entry == 16), 1.0, 0.0)
         for k, d in enumerate((d1, d2, d3)):
@@ -182,7 +192,8 @@
 
     for copy, offset in zip(halo, order):
         copy.wait_recv()
-        build(offset, (me + offset) % RING)
+        if offset:
+            build(offset, (me + offset) % RING)
 
     def contract(m, slots):
         far = (core + as_int(disp[m, 2] == 3)) % 2
@@ -199,46 +210,68 @@
                 left, jnp.concatenate(parts, axis=1), NT, preferred_element_type=jnp.float32)
             total = product if total is None else total + product
         rows_each = 4 * block
-        return [total[k * rows_each:(k + 1) * rows_each].reshape(4, block, 2 * vectors) for k in range(2)]
-
-    def carry(lane, step, source, peer):
+        return [total[k * rows_each:(k + 1) * rows_each].reshape(4, block, 2 * vectors) for k in range(len(slots))]
+
+    def carry(lane, step, part, peer):
+        rows_part = pl.ds(part * (4 // PARTS), 4 // PARTS)
         return pltpu.make_async_remote_copy(
-            src_ref=put.at[lane, step], dst_ref=got.at[lane, step],
-            send_sem=sum_send.at[lane, step], recv_sem=sum_recv.at[lane, step], device_id={"site": peer})
-
-    up = [carry(0, step, None, after) for step in range(3)]
-    down = [carry(1, step, None, behind) for step in range(3)]
-
-    across, below = contract(0, (2, 3))
+            src_ref=put.at[lane, step, rows_part], dst_ref=got.at[lane, step, rows_part],
+            send_sem=sum_send.at[lane, step, part], recv_sem=sum_recv.at[lane, step, part],
+            device_id={"site": peer})
+
+    up = [[carry(0, step, part, after) for part in range(PARTS)] for step in range(3)]
+    down = [[carry(1, step, part, behind) for part in range(PARTS)] for step in range(3)]
+
+    def send(copies):
+        for copy in copies:
+            copy.start()
+
+    pl.semaphore_wait(ready, 1)
+    across, = contract(0, (2,))
     put[0, 0] = across.astype(jnp.bfloat16)
-    up[0].start()
+    send(up[0])
+    across, = contract(1, (2,))
+    put[1, 0] = across.astype(jnp.bfloat16)
+    send(down[0])
+    above, = contract(1, (1,))
+    put[0, 1] = above.astype(jnp.bfloat16)
+    send(up[1])
+    below, = contract(0, (3,))
     put[1, 1] = below.astype(jnp.bfloat16)
-    across, above = contract(1, (2, 1))
-    put[1, 0] = across.astype(jnp.bfloat16)
-    down[0].start()
-    put[0, 1] = above.astype(jnp.bfloat16)
-    up[1].start()
-    down[1].start()
+    send(down[1])
+    build(0, me)
     above, own = contract(0, (1, 0))
     out[0] = own
-    up[0].wait_recv()
-    put[0, 2] = (above + got[0, 0].astype(jnp.float32)).astype(jnp.bfloat16)
-    up[2].start()
+    held[0] = above
     below, own = contract(1, (3, 0))
     out[1] = own
-    down[0].wait_recv()
-    put[1, 2] = (below + got[1, 0].astype(jnp.float32)).astype(jnp.bfloat16)
-    down[2].start()
-    up[1].wait_recv()
-    out[1] += got[0, 1].astype(jnp.float32)
-    down[1].wait_recv()
-    out[0] += got[1, 1].astype(jnp.float32)
-    up[2].wait_recv()
-    out[0] += got[0, 2].astype(jnp.float32)
-    down[2].wait_recv()
-    out[1] += got[1, 2].astype(jnp.float32)
-    for copy in halo + [small] + up + down:
+    held[1] = below
+    each = 4 // PARTS
+    for part in range(PARTS):
+        these = slice(part * each, part * each + each)
+        for lane, lines in ((0, up), (1, down)):
+            lines[0][part].wait_recv()
+            put[lane, 2, these] = (held[lane, these] + got[lane, 0, these].astype(jnp.float32)).astype(jnp.bfloat16)
+            lines[2][part].start()
+    for part in range(PARTS):
+        these = slice(part * each, part * each + each)
+        for lane, lines in ((0, up), (1, down)):
+            lines[1][part].wait_recv()
+            out[1 - lane, these] += got[lane, 1, these].astype(jnp.float32)
+    for part in range(PARTS):
+        these = slice(part * each, part * each + each)
+        for lane, lines in ((0, up), (1, down)):
+            lines[2][part].wait_recv()
+            out[lane, these] += got[lane, 2, these].astype(jnp.float32)
+    for copy in halo + small[:1]:
         copy.wait_send()
+    for lines in up + down:
+        for copy in lines:
+            copy.wait_send()
+
+    @pl.when(core == 1)
+    def _():
+        small[1].wait_send()
 
 
 def on_device(eigenvectors, gauge_links, displacements, block_rows):
@@ -251,7 +284,7 @@
     hbm = pl.BlockSpec(memory_space=pltpu.HBM)
     return pl.pallas_call(
         functools.partial(kernel, scale),
-        out_shape=jax.ShapeDtypeStruct((2, 4, block, 2 * vectors), f32),
+        out_shape=pltpu.VMEM((2, 4, block, 2 * vectors), f32),
         in_specs=[hbm, hbm, hbm, hbm],
         out_specs=pl.BlockSpec(memory_space=pltpu.VMEM),
         scratch_shapes=[
@@ -259,8 +292,9 @@
             pltpu.SMEM(block_rows.shape, block_rows.dtype),
             pltpu.VMEM(links.shape, bf16),
             pltpu.VMEM((2, RING, 2, 3, block, sites), bf16),
-            pltpu.VMEM((2, SMALL_ROWS, sites), bf16),
-            pltpu.VMEM((SMALL_ROWS, sites), f32),
+            pltpu.VMEM((2, 24, sites), bf16),
+            pltpu.VMEM((2, TABLE_ROWS, sites), bf16),
+            pltpu.VMEM((TABLE_ROWS, sites), f32),
             pltpu.VMEM((3, 24, sites), f32),
             pltpu.VMEM((24, sites), f32),
             pltpu.VMEM((2, 3, 3, 2, 8, sites), f32),
@@ -269,14 +303,16 @@
             pltpu.VMEM((2, 3, sites, sites), bf16),
             pltpu.VMEM((2, 3, 4, block, 2 * vectors), bf16),
             pltpu.VMEM((2, 3, 4, block, 2 * vectors), bf16),
+            pltpu.VMEM((2, 4, block, 2 * vectors), f32),
             pltpu.SemaphoreType.DMA((RING + 3,)),
-            pltpu.SemaphoreType.DMA((RING + 1,)),
-            pltpu.SemaphoreType.DMA((RING + 1,)),
-            pltpu.SemaphoreType.DMA((2, 3)),
-            pltpu.SemaphoreType.DMA((2, 3)),
+            pltpu.SemaphoreType.DMA((RING + 2,)),
+            pltpu.SemaphoreType.DMA((RING + 2,)),
+            pltpu.SemaphoreType.DMA((2, 3, PARTS)),
+            pltpu.SemaphoreType.DMA((2, 3, PARTS)),
+            pltpu.SemaphoreType.REGULAR,
         ],
         compiler_params=pltpu.CompilerParams(
-            collective_id=0, has_side_effects=True, vmem_limit_bytes=63 * 1024 * 1024 + 512 * 1024),
+            collective_id=0, has_side_effects=True, vmem_limit_bytes=62 * 1024 * 1024 + 512 * 1024),
     )(displacements, block_rows, psi, links)
 
 

time: 47.7 us -> 44.3 us (0.929)
  the two profiles are of different devices: /device:TPU:10 before, /device:TPU:1 now
where the time goes in v2:
time: 44.3 us; the launch traced here: 43.5 us
  Pallas kernels  42.7 us (96%)
  local copies, waits for them, and re-layouts  0.82 us (2%)
    pallas_call x1, Pallas kernels, on_device(): pl.pallas_call(functools.partial(kernel, scale), out_shape=pltpu.VMEM((2,...  42.7 us

profile of v2, /device:TPU:1, one launch (start us, length us, event | category | flops | bytes accessed | tf_op | source)
XLA Modules:
  0.0 43.5 jit_solution(2328439788243438946)
XLA Ops:
  0.0 42.7 %shard_map.46 = f32[2,4,48,384]{3,2,1,0:T(8,128)S(1)} custom-call(s32[2,3]{1,0:T(2,128)} %disp_hbm.1, s32[4]{0:T(128)} %rows_hbm.1, bf16[2,3,192,256]{3,2,1,0:T(8,128)(2,1)} %bitcast.6, bf16[3,3,3,2,256]{4,3,2,1,0:T(2,128)(2,1)} %bitcast.7), custom_call_target="tpu_custom_call" | custom-call | tf_op jit(solution)/shard_map/pallas_call | solution.py:285
  42.7 0.8 %copy.6 = f32[2,4,48,384]{3,2,1,0:T(8,128)} copy(f32[2,4,48,384]{3,2,1,0:T(8,128)S(1)} %shard_map.46) | data formatting | bytes 1179648

commit v3 on v2

--- a/solution.py
+++ b/solution.py
@@ -48,6 +48,11 @@
     after, behind = (me + 1) % RING, (me + RING - 1) % RING
     block = g.shape[4]
     sites = g.shape[5]
+
+    reader = (me + RING - 1 + 2 * core) % RING
+    writer = (me + 1 + 2 * core) % RING
+    barrier = pltpu.get_barrier_semaphore()
+    pl.semaphore_signal(barrier, inc=1, device_id={"site": writer})
 
     fills = [
         pltpu.make_async_copy(psi.at[:, :, pl.ds(chunk * block, block), :], g.at[0, chunk], local_sem.at[chunk])
@@ -58,21 +63,6 @@
     fills.append(pltpu.make_async_copy(disp_hbm, disp, local_sem.at[RING + 2]))
     for fill in fills:
         fill.start()
-    reader = (me + RING - 1 + 2 * core) % RING
-    writer = (me + 1 + 2 * core) % RING
-    barrier = pltpu.get_barrier_semaphore()
-    pl.semaphore_signal(barrier, inc=1, device_id={"site": writer})
-    pl.semaphore_wait(barrier, 1)
-    pl.semaphore_signal(ready, inc=1, device_id={"site": reader})
-
-    order = (2, 3, 1, 0)
-    halo = []
-    for number, offset in enumerate(order):
-        sent = (reader + offset) % RING
-        halo.append(pltpu.make_async_remote_copy(
-            src_ref=psi.at[:, :, pl.ds(pl.multiple_of(sent * block, block), block), :], dst_ref=g.at[1, sent],
-            send_sem=halo_send.at[number], recv_sem=halo_recv.at[number], device_id={"site": reader}))
-    halo[0].start()
     for fill in fills:
         fill.wait()
 
@@ -97,6 +87,17 @@
             picked += jnp.dot(pick, whole, preferred_element_type=jnp.float32)
     lb[0] = picked.astype(jnp.bfloat16)
     kb[0] = s32[...].astype(jnp.bfloat16)
+    pl.semaphore_wait(barrier, 1)
+    pl.semaphore_signal(ready, inc=1, device_id={"site": reader})
+
+    order = (2, 3, 1, 0)
+    halo = []
+    for number, offset in enumerate(order):
+        sent = (reader + offset) % RING
+        halo.append(pltpu.make_async_remote_copy(
+            src_ref=psi.at[:, :, pl.ds(pl.multiple_of(sent * block, block), block), :], dst_ref=g.at[1, sent],
+            send_sem=halo_send.at[number], recv_sem=halo_recv.at[number], device_id={"site": reader}))
+
     small = [pltpu.make_async_remote_copy(
         src_ref=buffer.at[0], dst_ref=buffer.at[1],
         send_sem=halo_send.at[RING + number], recv_sem=halo_recv.at[RING + number], device_id={"site": reader})
@@ -107,7 +108,7 @@
     def _():
         small[1].start()
 
-    for copy in halo[1:]:
+    for copy in halo:
         copy.start()
 
     for m in range(2):

time: 44.3 us -> 43.9 us (level); the launches traced: 43.5 us -> 43.8 us
  no operation moved by 1% of the time
where the time goes in v3:
time: 43.9 us; the launch traced here: 43.8 us
  Pallas kernels  43 us (98%)
  local copies, waits for them, and re-layouts  0.82 us (2%)
    pallas_call x1, Pallas kernels, on_device(): pl.pallas_call(functools.partial(kernel, scale), out_shape=pltpu.VMEM((2,...  43 us

profile of v3, /device:TPU:1, one launch (start us, length us, event | category | flops | bytes accessed | tf_op | source)
XLA Modules:
  0.0 43.8 jit_solution(14551097629243261881)
XLA Ops:
  0.0 43.0 %shard_map.46 = f32[2,4,48,384]{3,2,1,0:T(8,128)S(1)} custom-call(s32[2,3]{1,0:T(2,128)} %disp_hbm.1, s32[4]{0:T(128)} %rows_hbm.1, bf16[2,3,192,256]{3,2,1,0:T(8,128)(2,1)} %bitcast.6, bf16[3,3,3,2,256]{4,3,2,1,0:T(2,128)(2,1)} %bitcast.7), custom_call_target="tpu_custom_call" | custom-call | tf_op jit(solution)/shard_map/pallas_call | solution.py:286
  43.0 0.8 %copy.6 = f32[2,4,48,384]{3,2,1,0:T(8,128)} copy(f32[2,4,48,384]{3,2,1,0:T(8,128)S(1)} %shard_map.46) | data formatting | bytes 1179648

commit v4 on v3

--- a/solution.py
+++ b/solution.py
@@ -58,7 +58,7 @@
         pltpu.make_async_copy(psi.at[:, :, pl.ds(chunk * block, block), :], g.at[0, chunk], local_sem.at[chunk])
         for chunk in range(RING)
     ]
-    fills.append(pltpu.make_async_copy(links_hbm, links, local_sem.at[RING]))
+    fills.append(pltpu.make_async_copy(links_hbm, links.at[0], local_sem.at[RING]))
     fills.append(pltpu.make_async_copy(rows_hbm, rows, local_sem.at[RING + 1]))
     fills.append(pltpu.make_async_copy(disp_hbm, disp, local_sem.at[RING + 2]))
     for fill in fills:
@@ -66,12 +66,6 @@
     for fill in fills:
         fill.wait()
 
-    s32[3 * LINK_ROWS:] = jnp.zeros((TABLE_ROWS - 3 * LINK_ROWS, sites), jnp.float32)
-    for direction in range(3):
-        for a in range(3):
-            for b in range(3):
-                at = direction * LINK_ROWS + (a * 3 + b) * 2
-                s32[at:at + 2] = links[direction, a, b].astype(jnp.float32)
     vectors = RING * block
     number = lax.broadcasted_iota(jnp.int32, (24, vectors), 0)
     column = lax.broadcasted_iota(jnp.int32, (24, vectors), 1)
@@ -86,7 +80,6 @@
             whole = jnp.concatenate([g[0, chunk, q, c] for chunk in range(RING)], axis=0)
             picked += jnp.dot(pick, whole, preferred_element_type=jnp.float32)
     lb[0] = picked.astype(jnp.bfloat16)
-    kb[0] = s32[...].astype(jnp.bfloat16)
     pl.semaphore_wait(barrier, 1)
     pl.semaphore_signal(ready, inc=1, device_id={"site": reader})
 
@@ -95,13 +88,13 @@
     for number, offset in enumerate(order):
         sent = (reader + offset) % RING
         halo.append(pltpu.make_async_remote_copy(
-            src_ref=psi.at[:, :, pl.ds(pl.multiple_of(sent * block, block), block), :], dst_ref=g.at[1, sent],
+            src_ref=g.at[0, sent], dst_ref=g.at[1, sent],
             send_sem=halo_send.at[number], recv_sem=halo_recv.at[number], device_id={"site": reader}))
 
     small = [pltpu.make_async_remote_copy(
         src_ref=buffer.at[0], dst_ref=buffer.at[1],
         send_sem=halo_send.at[RING + number], recv_sem=halo_recv.at[RING + number], device_id={"site": reader})
-        for number, buffer in enumerate((lb, kb))]
+        for number, buffer in enumerate((lb, links))]
     small[0].start()
 
     @pl.when(core == 1)
@@ -124,12 +117,20 @@
     def _():
         small[1].wait_recv()
 
+    s32[3 * LINK_ROWS:] = jnp.zeros((TABLE_ROWS - 3 * LINK_ROWS, sites), jnp.float32)
+    for direction in range(3):
+        for a in range(3):
+            for b in range(3):
+                at = direction * LINK_ROWS + (a * 3 + b) * 2
+                s32[at:at + 2] = links[core, direction, a, b].astype(jnp.float32)
+    kb[...] = s32[...].astype(jnp.bfloat16)
+
     def imported(d):
         return (core + as_int(d == 3)) % 2 == 1
 
     def weights(m, carried):
         d1, d2, d3 = disp[m, 0], disp[m, 1], disp[m, 2]
-        moved = jnp.dot(kb[core], perm[m, 0], preferred_element_type=jnp.float32)
+        moved = jnp.dot(kb[...], perm[m, 0], preferred_element_type=jnp.float32)
         left = lb[(core + as_int(d1 == 3)) % 2]
         entry = lax.broadcasted_iota(jnp.int32, (LINK_ROWS, sites), 0)
         identity = jnp.where((entry == 0) | (entry == 8) | (entry == 16), 1.0, 0.0)
@@ -291,10 +292,10 @@
         scratch_shapes=[
             pltpu.SMEM(displacements.shape, displacements.dtype),
             pltpu.SMEM(block_rows.shape, block_rows.dtype),
-            pltpu.VMEM(links.shape, bf16),
+            pltpu.VMEM((2,) + links.shape, bf16),
             pltpu.VMEM((2, RING, 2, 3, block, sites), bf16),
             pltpu.VMEM((2, 24, sites), bf16),
-            pltpu.VMEM((2, TABLE_ROWS, sites), bf16),
+            pltpu.VMEM((TABLE_ROWS, sites), bf16),
             pltpu.VMEM((TABLE_ROWS, sites), f32),
             pltpu.VMEM((3, 24, sites), f32),
             pltpu.VMEM((24, sites), f32),

time: 43.9 us -> 43.8 us (level)
  no operation moved by 1% of the time
where the time goes in v4:
time: 43.8 us; the launch traced here: 43.7 us
  Pallas kernels  42.9 us (98%)
  local copies, waits for them, and re-layouts  0.82 us (2%)
    pallas_call x1, Pallas kernels, on_device(): pl.pallas_call(functools.partial(kernel, scale), out_shape=pltpu.VMEM((2,...  42.9 us

profile of v4, /device:TPU:1, one launch (start us, length us, event | category | flops | bytes accessed | tf_op | source)
XLA Modules:
  0.0 43.7 jit_solution(15412055044528016146)
XLA Ops:
  0.0 42.9 %shard_map.46 = f32[2,4,48,384]{3,2,1,0:T(8,128)S(1)} custom-call(s32[2,3]{1,0:T(2,128)} %disp_hbm.1, s32[4]{0:T(128)} %rows_hbm.1, bf16[2,3,192,256]{3,2,1,0:T(8,128)(2,1)} %bitcast.6, bf16[3,3,3,2,256]{4,3,2,1,0:T(2,128)(2,1)} %bitcast.7), custom_call_target="tpu_custom_call" | custom-call | tf_op jit(solution)/shard_map/pallas_call | solution.py:287
  42.9 0.8 %copy.6 = f32[2,4,48,384]{3,2,1,0:T(8,128)} copy(f32[2,4,48,384]{3,2,1,0:T(8,128)S(1)} %shard_map.46) | data formatting | bytes 1179648
